TPU v7x, 32 devices: a whole 2x2x4 slice. The times are simulated.
32 devices in a mesh: row: 4 (over z), col: 8 (over y, x, core).
Axes of the slice: x: 2, y: 2, z: 4, core: 2. Of those that a mesh axis runs over, the one named last changes fastest.
Arguments:
- examples: bfloat16 [65536, 1024], P(('row', 'col')), may hold values from -20 to 20
- residuals: float32 [65536, 256], P(('row', 'col')), may hold values from -6 to 6
- coefficients: float32 [65536, 256], P(('row', 'col')), may hold values from -0.8 to 0.8
- block_index: int32 [1], replicated, may hold values from 0 to 63
Outputs:
- new_residuals: float32 [65536, 256], P(('row', 'col'))
- new_coefficients: float32 [65536, 256], P(('row', 'col'))
All inputs are finite; a program needn't handle non-finite values.
Results may differ from a plain program's by a relative error of at most 0.00035.
Values may be sent and summed in bfloat16 or wider, within the bound.
No kernel may reach another device: no remote copies, remote signals or barrier semaphores. Data moves between devices by JAX's collectives and lax.ppermute only.
A program may use at most 128 MiB of HBM per device.

v0:
```python
import jax
import jax.numpy as jnp
from jax import lax
from jax.sharding import PartitionSpec as P

BLOCK = 1024
ridge = 0.001
width_factor = 0.5


def spread(value, axis, source):
    kept = jnp.where(lax.axis_index(axis) == source, value, 0).astype(value.dtype)
    return lax.psum(kept, axis)


def body(examples, residuals, coefficients, block_index):
    rows_here = examples.shape[0]
    features = examples.shape[1]
    per_device = rows_here // BLOCK
    devices_all = lax.axis_size(("row", "col"))
    total_examples = rows_here * devices_all
    chosen = block_index[0]
    owner_rank = chosen // per_device
    offset = chosen % per_device * BLOCK
    my_rank = lax.axis_index(("row", "col"))
    is_owner = owner_rank == my_rank
    my_block = lax.dynamic_slice_in_dim(examples, offset, BLOCK, 0)
    block_rows = spread(my_block, ("row", "col"), owner_rank)
    sq_rows = jnp.sum(jnp.square(examples.astype(jnp.float32)), axis=1)
    sq_block = jnp.sum(jnp.square(block_rows.astype(jnp.float32)), axis=1)
    inner = lax.dot_general(
        examples, block_rows, (((1,), (1,)), ((), ())), preferred_element_type=jnp.float32
    )
    kernel = jnp.exp(
        -width_factor * (sq_rows[:, None] + sq_block[None, :] - 2.0 * inner) / features
    ).astype(jnp.bfloat16)
    residual_low = residuals.astype(jnp.bfloat16)
    grad_part = lax.dot_general(
        kernel, residual_low, (((0,), (0,)), ((), ())), preferred_element_type=jnp.float32
    )
    gram_part = lax.dot_general(
        kernel, kernel, (((0,), (0,)), ((), ())), preferred_element_type=jnp.float32
    )
    own_coef = lax.dynamic_slice_in_dim(coefficients, offset, BLOCK, 0)
    weight_own = jnp.where(is_owner, total_examples * ridge, 0.0).astype(jnp.float32)
    grad_part = grad_part - weight_own * own_coef
    grad, gram_sum = lax.psum((grad_part, gram_part), ("row", "col"))
    system = gram_sum / total_examples + ridge * jnp.eye(BLOCK, dtype=jnp.float32)
    factor = jnp.linalg.cholesky(system)
    update = jax.scipy.linalg.cho_solve((factor, True), grad / total_examples)
    update_low = update.astype(jnp.bfloat16)
    new_residuals = residuals - jnp.dot(kernel, update_low, preferred_element_type=jnp.float32)
    updated = lax.dynamic_update_slice_in_dim(coefficients, own_coef + update, offset, 0)
    new_coefficients = jnp.where(is_owner, updated, coefficients)
    return (new_residuals, new_coefficients)


def solution(mesh):
    in_specs = (P(("row", "col"), None), P(("row", "col"), None), P(("row", "col"), None), P())
    out_specs = (P(("row", "col"), None), P(("row", "col"), None))
    return jax.shard_map(body, mesh=mesh, in_specs=in_specs, out_specs=out_specs, check_vma=False)
```

profile of v0, /device:TPU:0, one launch (start us, length us, event | category | flops | bytes accessed | tf_op | source)
XLA Modules:
  0.0 689.6 jit_solution(11509813493711825370)
XLA Ops:
  9.5 3.4 dynamic-slice_select_fusion
  13.0 3.1 multiply_reduce_fusion
  16.1 135.1 %all-reduce.5.cloned.1.call-done = bf16[1024,1024]{1,0:T(8,128)(2,1)} async-done(((bf16[1024,1024]{1,0:T(8,128)(2,1)}), bf16[1024,1024]{1,0:T(8,128)(2,1)}) %all-reduce.5.cloned.1.call-update) | async-done | bytes 2097168 | tf_op jit(solution)/shard_map/psum | solution.py:13
  153.3 7.9 %fusion.2 = bf16[2048,1024]{0,1:T(8,128)(2,1)S(1)} fusion(bf16[1024,1024]{1,0:T(8,128)(2,1)} %all-reduce.5.cloned.1.call-done, bf16[2048,1024]{1,0:T(8,128)(2,1)} %param.4, f32[1024]{0:T(1024)S(1)} %multiply_reduce_fusion.1, f32[2048]{0:T(1024)S(1)} %multiply_reduce_fusion), kind=kOutput, calls=%fused_computation.5 | convolution fusion | flops 4305453056 | bytes 10498048 | tf_op jit(solution)/shard_map/dot_general | solution.py:31
  161.2 6.1 fusion.101
  169.5 147.1 %all-reduce.7.cloned.1.call-done = (f32[1024,256]{1,0:T(8,128)}, f32[1024,1024]{0,1:T(8,128)}) async-done(((f32[1024,256]{1,0:T(8,128)}, f32[1024,1024]{0,1:T(8,128)}), (f32[1024,256]{1,0:T(8,128)}, f32[1024,1024]{0,1:T(8,128)})) %all-reduce.7.cloned.1.call-update) | async-done | bytes 5242896 | tf_op jit(solution)/shard_map/psum | solution.py:47
  316.6 5.0 select_add_fusion
  321.6 5.5 copy.7
  327.1 4.5 fusion.3
  333.5 11.7 %cholesky.222 = f32[128,128]{1,0:T(8,128)S(1)} custom-call(f32[128,128]{1,0:T(8,128)S(1)} %cholesky.577), custom_call_target="Cholesky" | custom-call | tf_op jit(solution)/shard_map/jit(cholesky)/cholesky | solution.py:49
  345.4 9.8 %custom-call.66 = f32[1,128,128]{1,2,0:T(8,128)S(1)} custom-call(f32[1,128,128]{2,1,0:T(8,128)S(1)} %get-tuple-element.56), custom_call_target="InvertDiagBlocksLowerTriangular" | custom-call | tf_op jit(solution)/shard_map/jit(cholesky)/cholesky | solution.py:49
  359.3 11.7 %cholesky.243 = f32[128,128]{1,0:T(8,128)S(1)} custom-call(f32[128,128]{1,0:T(8,128)S(1)} %cholesky.581), custom_call_target="Cholesky" | custom-call | tf_op jit(solution)/shard_map/jit(cholesky)/cholesky | solution.py:49
  373.8 9.8 %custom-call.67 = f32[1,128,128]{1,2,0:T(8,128)S(1)} custom-call(f32[1,128,128]{2,1,0:T(8,128)S(1)} %get-tuple-element.54), custom_call_target="InvertDiagBlocksLowerTriangular" | custom-call | tf_op jit(solution)/shard_map/jit(cholesky)/cholesky | solution.py:49
  389.2 11.7 %cholesky.466 = f32[128,128]{1,0:T(8,128)S(1)} custom-call(f32[128,128]{1,0:T(8,128)S(1)} %cholesky.586), custom_call_target="Cholesky" | custom-call | tf_op jit(solution)/shard_map/jit(cholesky)/cholesky | solution.py:49
  401.7 9.8 %custom-call.68 = f32[1,128,128]{1,2,0:T(8,128)S(1)} custom-call(f32[1,128,128]{2,1,0:T(8,128)S(1)} %get-tuple-element.52), custom_call_target="InvertDiagBlocksLowerTriangular" | custom-call | tf_op jit(solution)/shard_map/jit(cholesky)/cholesky | solution.py:49
  412.7 3.5 convolution_subtract_fusion.4
  416.3 11.7 %cholesky.485 = f32[128,128]{1,0:T(8,128)S(1)} custom-call(f32[128,128]{1,0:T(8,128)S(1)} %cholesky.591), custom_call_target="Cholesky" | custom-call | tf_op jit(solution)/shard_map/jit(cholesky)/cholesky | solution.py:49
  428.7 9.8 %custom-call.69 = f32[1,128,128]{1,2,0:T(8,128)S(1)} custom-call(f32[1,128,128]{2,1,0:T(8,128)S(1)} %get-tuple-element.50), custom_call_target="InvertDiagBlocksLowerTriangular" | custom-call | tf_op jit(solution)/shard_map/jit(cholesky)/cholesky | solution.py:49
  439.7 3.2 convolution_subtract_fusion.5
  442.9 11.9 %cholesky.504 = f32[128,128]{1,0:T(8,128)S(1)} custom-call(f32[128,128]{1,0:T(8,128)S(1)} %cholesky.596), custom_call_target="Cholesky" | custom-call | tf_op jit(solution)/shard_map/jit(cholesky)/cholesky | solution.py:49
  455.5 9.8 %custom-call.70 = f32[1,128,128]{1,2,0:T(8,128)S(1)} custom-call(f32[1,128,128]{2,1,0:T(8,128)S(1)} %get-tuple-element.48), custom_call_target="InvertDiagBlocksLowerTriangular" | custom-call | tf_op jit(solution)/shard_map/jit(cholesky)/cholesky | solution.py:49
  466.5 3.2 convolution_subtract_fusion.6
  469.7 11.7 %cholesky.524 = f32[128,128]{1,0:T(8,128)S(1)} custom-call(f32[128,128]{1,0:T(8,128)S(1)} %cholesky.601), custom_call_target="Cholesky" | custom-call | tf_op jit(solution)/shard_map/jit(cholesky)/cholesky | solution.py:49
  482.2 9.8 %custom-call.71 = f32[1,128,128]{1,2,0:T(8,128)S(1)} custom-call(f32[1,128,128]{2,1,0:T(8,128)S(1)} %get-tuple-element.46), custom_call_target="InvertDiagBlocksLowerTriangular" | custom-call | tf_op jit(solution)/shard_map/jit(cholesky)/cholesky | solution.py:49
  493.0 3.1 convolution_subtract_fusion.19
  496.2 11.7 %cholesky.544 = f32[128,128]{1,0:T(8,128)S(1)} custom-call(f32[128,128]{1,0:T(8,128)S(1)} %cholesky.606), custom_call_target="Cholesky" | custom-call | tf_op jit(solution)/shard_map/jit(cholesky)/cholesky | solution.py:49
  508.6 9.8 %custom-call.72 = f32[1,128,128]{1,2,0:T(8,128)S(1)} custom-call(f32[1,128,128]{2,1,0:T(8,128)S(1)} %get-tuple-element.44), custom_call_target="InvertDiagBlocksLowerTriangular" | custom-call | tf_op jit(solution)/shard_map/jit(cholesky)/cholesky | solution.py:49
  521.6 11.7 %cholesky.562 = f32[128,128]{1,0:T(8,128)S(1)} custom-call(f32[128,128]{1,0:T(8,128)S(1)} %convolution_subtract_fusion.22), custom_call_target="Cholesky" | custom-call | tf_op jit(solution)/shard_map/jit(cholesky)/cholesky | solution.py:49
  545.0 4.9 select_select_fusion
  549.9 28.3 %while.1 = (s32[]{:T(128)}, f32[1024,1024]{0,1:T(8,128)}, s32[8,2]{0,1:T(2,128)S(1)}, f32[8,128,128]{2,1,0:T(8,128)}, s32[]{:T(128)}) while((s32[]{:T(128)}, f32[1024,1024]{0,1:T(8,128)}, s32[8,2]{0,1:T(2,128)S(1)}, f32[8,128,128]{2,1,0:T(8,128)}, s32[]{:T(128)}) %tuple.53), condition=%wide.while_cond, body=%wide.while_body.sunk | while | flops 2 | bytes 393329 | solution.py:50
  578.2 80.2 %custom-call.73 = f32[8,128,128]{1,2,0:T(8,128)} custom-call(f32[8,128,128]{2,1,0:T(8,128)} %get-tuple-element.9), custom_call_target="InvertDiagBlocksLowerTriangular" | custom-call | tf_op jit(solution)/shard_map/jit(_cho_solve)/triangular_solve | solution.py:50
  678.2 2.8 convolution_subtract_fusion
  (174 shorter events, 87.9 us)
Async XLA Ops:
  7.2 144.0 %all-reduce.5.cloned.1.call-start = ((), (), s32[]{:S(2)}) async-start(), calls=%async_computation | async-start | bytes 4194304 | tf_op jit(solution)/shard_map/psum | solution.py:13
  13.0 303.6 %all-reduce.7.cloned.1.call-start = ((), (), s32[]{:S(2)}) async-start(), calls=%async_computation.1 | async-start | bytes 10485760 | tf_op jit(solution)/shard_map/psum | solution.py:47
  161.1 6.1 copy-start.2
  161.1 6.1 copy-start.5
  331.5 2.0 copy-start.1
  358.5 0.8 copy-start.8
  359.3 25.9 %copy-start.9 = (f32[896,128]{1,0:T(8,128)S(1)}, f32[896,128]{1,0:T(8,128)}, u32[]{:S(2)}) copy-start(f32[896,128]{1,0:T(8,128)} %copy-done.8) | copy-start | bytes 1376260
  658.4 8.8 %copy-start = (f32[1024,1024]{0,1:T(8,128)S(1)}, f32[1024,1024]{0,1:T(8,128)}, u32[]{:S(2)}) copy-start(f32[1024,1024]{0,1:T(8,128)} %get-tuple-element.124) | copy-start | bytes 12582916
  658.4 9.5 %copy-start.7 = (f32[8,128,128]{1,2,0:T(8,128)S(1)}, f32[8,128,128]{1,2,0:T(8,128)}, u32[]{:S(2)}) copy-start(f32[8,128,128]{1,2,0:T(8,128)} %custom-call.73) | copy-start | bytes 1572868
  675.4 2.2 copy-start.3
  675.4 2.9 copy-start.6
  681.2 1.3 copy-start.4
Sparse Core Ops, SparseCore 0:
  13.9 137.2 all-reduce.4
  169.6 146.9 all-reduce.6
where the time goes:
time: 698 us; the launch traced here: 690 us
  waiting for transfers between devices  282 us (40%)
  other arithmetic  272 us (39%)
  matrix products  65 us (9%)
  local copies, waits for them, and re-layouts  49.5 us (7%)
  between operations  20.7 us (3%)
    another operation x30, other arithmetic, body(): factor = jnp.linalg.cholesky(system)  167 us
    psum x1, waiting for transfers between devices, body(): grad, gram_sum = lax.psum((grad_part, gram_part), ('row', 'col'))  147 us
    psum x1, waiting for transfers between devices, spread(): return lax.psum(kept, axis)  135 us
    another operation x3, other arithmetic, body(): update = jax.scipy.linalg.cho_solve((factor, True), grad / total_examples)  85.1 us
    another operation x40, local copies, waits for them, and re-layouts  28.2 us
    another operation x14, matrix products, body(): factor = jnp.linalg.cholesky(system)  27.7 us
    another operation x30, matrix products, body(): update = jax.scipy.linalg.cho_solve((factor, True), grad / total_examples)  18.3 us
  transfers between devices with their start and end apart: 2, of which 2 were waited for; matrix products, arithmetic and copies ran while one was open for 0% of the time, Pallas kernels for 0%

commit v1 on v0

--- a/solution.py
+++ b/solution.py
@@ -10,7 +10,7 @@
 
 def spread(value, axis, source):
     kept = jnp.where(lax.axis_index(axis) == source, value, 0).astype(value.dtype)
-    return lax.psum(kept, axis)
+    return jnp.sum(lax.all_gather(kept, axis), axis=0)
 
 
 def body(examples, residuals, coefficients, block_index):

time: 698 us -> 933 us (1.34)
  waiting for transfers between devices: 282 us -> 502 us
  other arithmetic: 272 us -> 292 us
    all_gather x0 -> x1, waiting for transfers between devices: none -> 355 us  [spread(): return jnp.sum(lax.all_gather(kept, axis), axis=0)]
    psum x1 -> x0, waiting for transfers between devices: 135 us -> none  [spread(): return lax.psum(kept, axis)]
    reduce_sum x0 -> x1, other arithmetic: none -> 21.3 us  [spread(): return jnp.sum(lax.all_gather(kept, axis), axis=0)]
where the time goes in v1:
time: 933 us; the launch traced here: 925 us
  waiting for transfers between devices  502 us (54%)
  other arithmetic  292 us (31%)
  matrix products  59.7 us (6%)
  local copies, waits for them, and re-layouts  50.6 us (5%)
  between operations  20.7 us (2%)
    all_gather x1, waiting for transfers between devices, spread(): return jnp.sum(lax.all_gather(kept, axis), axis=0)  355 us
    another operation x30, other arithmetic, body(): factor = jnp.linalg.cholesky(system)  168 us
    psum x1, waiting for transfers between devices, body(): grad, gram_sum = lax.psum((grad_part, gram_part), ('row', 'col'))  147 us
    another operation x3, other arithmetic, body(): update = jax.scipy.linalg.cho_solve((factor, True), grad / total_examples)  84.5 us
    another operation x40, local copies, waits for them, and re-layouts  28.2 us
    another operation x14, matrix products, body(): factor = jnp.linalg.cholesky(system)  27.3 us
    reduce_sum x1, other arithmetic, spread(): return jnp.sum(lax.all_gather(kept, axis), axis=0)  21.3 us
  transfers between devices with their start and end apart: 2, of which 2 were waited for; matrix products, arithmetic and copies ran while one was open for 0% of the time, Pallas kernels for 0%

profile of v1, /device:TPU:0, one launch (start us, length us, event | category | flops | bytes accessed | tf_op | source)
XLA Modules:
  0.0 924.7 jit_solution(12574962738448029715)
XLA Ops:
  7.2 3.0 copy.116
  10.9 3.4 dynamic-slice_select_fusion
  14.5 3.1 multiply_reduce_fusion
  17.5 355.4 %all-gather.3.cloned.1.call-done = bf16[32768,1024]{1,0:T(8,128)(2,1)} async-done(((bf16[1024,1024]{1,0:T(8,128)(2,1)}), bf16[32768,1024]{1,0:T(8,128)(2,1)}) %all-gather.3.cloned.1.call-update) | async-done | bytes 67108880 | tf_op jit(solution)/shard_map/all_gather | solution.py:13
  372.9 21.3 %reduce_sum.31 = bf16[1024,1024]{1,0:T(8,128)(2,1)S(1)} reduce(bf16[32,1024,1024]{2,1,0:T(8,128)(2,1)} %bitcast.1, bf16[]{:T(256)} %constant.330.clone.1), dimensions={0}, to_apply=%region_1.2 | reduce | flops 32505856 | bytes 69206016 | tf_op jit(solution)/shard_map/reduce_sum | solution.py:13
  394.7 7.7 fusion.2
  402.5 6.1 fusion.101
  410.9 146.5 %all-reduce.4.cloned.1.call-done = (f32[1024,256]{1,0:T(8,128)}, f32[1024,1024]{0,1:T(8,128)}) async-done(((f32[1024,256]{1,0:T(8,128)}, f32[1024,1024]{0,1:T(8,128)}), (f32[1024,256]{1,0:T(8,128)}, f32[1024,1024]{0,1:T(8,128)})) %all-reduce.4.cloned.1.call-update) | async-done | bytes 5242896 | tf_op jit(solution)/shard_map/psum | solution.py:47
  557.4 5.0 select_add_fusion
  562.4 5.8 copy.25
  568.2 4.5 fusion.3
  574.7 11.7 %cholesky.222 = f32[128,128]{1,0:T(8,128)S(1)} custom-call(f32[128,128]{1,0:T(8,128)S(1)} %cholesky.577), custom_call_target="Cholesky" | custom-call | tf_op jit(solution)/shard_map/jit(cholesky)/cholesky | solution.py:49
  586.4 9.8 %custom-call.66 = f32[1,128,128]{1,2,0:T(8,128)S(1)} custom-call(f32[1,128,128]{2,1,0:T(8,128)S(1)} %get-tuple-element.60), custom_call_target="InvertDiagBlocksLowerTriangular" | custom-call | tf_op jit(solution)/shard_map/jit(cholesky)/cholesky | solution.py:49
  600.1 11.7 %cholesky.243 = f32[128,128]{1,0:T(8,128)S(1)} custom-call(f32[128,128]{1,0:T(8,128)S(1)} %cholesky.581), custom_call_target="Cholesky" | custom-call | tf_op jit(solution)/shard_map/jit(cholesky)/cholesky | solution.py:49
  614.9 9.8 %custom-call.67 = f32[1,128,128]{1,2,0:T(8,128)S(1)} custom-call(f32[1,128,128]{2,1,0:T(8,128)S(1)} %get-tuple-element.58), custom_call_target="InvertDiagBlocksLowerTriangular" | custom-call | tf_op jit(solution)/shard_map/jit(cholesky)/cholesky | solution.py:49
  630.3 11.7 %cholesky.466 = f32[128,128]{1,0:T(8,128)S(1)} custom-call(f32[128,128]{1,0:T(8,128)S(1)} %cholesky.586), custom_call_target="Cholesky" | custom-call | tf_op jit(solution)/shard_map/jit(cholesky)/cholesky | solution.py:49
  642.8 9.8 %custom-call.68 = f32[1,128,128]{1,2,0:T(8,128)S(1)} custom-call(f32[1,128,128]{2,1,0:T(8,128)S(1)} %get-tuple-element.56), custom_call_target="InvertDiagBlocksLowerTriangular" | custom-call | tf_op jit(solution)/shard_map/jit(cholesky)/cholesky | solution.py:49
  653.8 3.3 convolution_subtract_fusion.4
  657.2 11.7 %cholesky.485 = f32[128,128]{1,0:T(8,128)S(1)} custom-call(f32[128,128]{1,0:T(8,128)S(1)} %cholesky.591), custom_call_target="Cholesky" | custom-call | tf_op jit(solution)/shard_map/jit(cholesky)/cholesky | solution.py:49
  669.6 9.8 %custom-call.69 = f32[1,128,128]{1,2,0:T(8,128)S(1)} custom-call(f32[1,128,128]{2,1,0:T(8,128)S(1)} %get-tuple-element.54), custom_call_target="InvertDiagBlocksLowerTriangular" | custom-call | tf_op jit(solution)/shard_map/jit(cholesky)/cholesky | solution.py:49
  680.6 3.1 convolution_subtract_fusion.5
  683.8 12.1 %cholesky.504 = f32[128,128]{1,0:T(8,128)S(1)} custom-call(f32[128,128]{1,0:T(8,128)S(1)} %cholesky.596), custom_call_target="Cholesky" | custom-call | tf_op jit(solution)/shard_map/jit(cholesky)/cholesky | solution.py:49
  696.7 9.8 %custom-call.70 = f32[1,128,128]{1,2,0:T(8,128)S(1)} custom-call(f32[1,128,128]{2,1,0:T(8,128)S(1)} %get-tuple-element.52), custom_call_target="InvertDiagBlocksLowerTriangular" | custom-call | tf_op jit(solution)/shard_map/jit(cholesky)/cholesky | solution.py:49
  707.6 3.2 convolution_subtract_fusion.6
  710.8 11.7 %cholesky.524 = f32[128,128]{1,0:T(8,128)S(1)} custom-call(f32[128,128]{1,0:T(8,128)S(1)} %cholesky.601), custom_call_target="Cholesky" | custom-call | tf_op jit(solution)/shard_map/jit(cholesky)/cholesky | solution.py:49
  723.3 9.8 %custom-call.71 = f32[1,128,128]{1,2,0:T(8,128)S(1)} custom-call(f32[1,128,128]{2,1,0:T(8,128)S(1)} %get-tuple-element.50), custom_call_target="InvertDiagBlocksLowerTriangular" | custom-call | tf_op jit(solution)/shard_map/jit(cholesky)/cholesky | solution.py:49
  737.1 11.7 %cholesky.544 = f32[128,128]{1,0:T(8,128)S(1)} custom-call(f32[128,128]{1,0:T(8,128)S(1)} %cholesky.606), custom_call_target="Cholesky" | custom-call | tf_op jit(solution)/shard_map/jit(cholesky)/cholesky | solution.py:49
  749.5 9.8 %custom-call.72 = f32[1,128,128]{1,2,0:T(8,128)S(1)} custom-call(f32[1,128,128]{2,1,0:T(8,128)S(1)} %get-tuple-element.48), custom_call_target="InvertDiagBlocksLowerTriangular" | custom-call | tf_op jit(solution)/shard_map/jit(cholesky)/cholesky | solution.py:49
  762.5 11.7 %cholesky.562 = f32[128,128]{1,0:T(8,128)S(1)} custom-call(f32[128,128]{1,0:T(8,128)S(1)} %convolution_subtract_fusion.22), custom_call_target="Cholesky" | custom-call | tf_op jit(solution)/shard_map/jit(cholesky)/cholesky | solution.py:49
  784.6 4.9 select_select_fusion
  789.5 28.3 %while.1 = (s32[]{:T(128)}, f32[1024,1024]{0,1:T(8,128)}, s32[8,2]{0,1:T(2,128)S(1)}, f32[8,128,128]{2,1,0:T(8,128)}, s32[]{:T(128)}) while((s32[]{:T(128)}, f32[1024,1024]{0,1:T(8,128)}, s32[8,2]{0,1:T(2,128)S(1)}, f32[8,128,128]{2,1,0:T(8,128)}, s32[]{:T(128)}) %tuple.54), condition=%wide.while_cond, body=%wide.while_body.sunk | while | flops 2 | bytes 393829 | solution.py:50
  817.8 79.6 %custom-call.73 = f32[8,128,128]{1,2,0:T(8,128)S(1)} custom-call(f32[8,128,128]{2,1,0:T(8,128)} %get-tuple-element.9), custom_call_target="InvertDiagBlocksLowerTriangular" | custom-call | tf_op jit(solution)/shard_map/jit(_cho_solve)/triangular_solve | solution.py:50
  (175 shorter events, 85.2 us)
Async XLA Ops:
  7.2 365.8 %all-gather.3.cloned.1.call-start = ((), (), s32[]{:S(2)}) async-start(), calls=%async_computation | async-start | bytes 69206016 | tf_op jit(solution)/shard_map/all_gather | solution.py:13
  14.4 543.0 %all-reduce.4.cloned.1.call-start = ((), (), s32[]{:S(2)}) async-start(), calls=%async_computation.1 | async-start | bytes 10485760 | tf_op jit(solution)/shard_map/psum | solution.py:47
  402.5 6.1 copy-start.2
  402.5 6.1 copy-start.4
  402.5 6.1 copy-start.6
  572.7 2.0 copy-start.1
  599.3 0.8 copy-start.8
  612.3 13.9 %copy-start.9 = (f32[896,128]{1,0:T(8,128)S(1)}, f32[896,128]{1,0:T(8,128)}, u32[]{:S(2)}) copy-start(f32[896,128]{1,0:T(8,128)} %copy-done.8) | copy-start | bytes 1376260
  897.4 4.9 copy-start
  912.0 2.2 copy-start.3
  912.0 2.9 copy-start.7
  914.9 2.8 copy-start.5
Sparse Core Ops, SparseCore 0:
  14.5 358.3 all-gather.2
  411.0 146.3 all-reduce.3
